TPU v7x, 128 devices: a whole 4x4x4 slice. The times are simulated.
128 devices in a mesh: inst: 4 (over x_hi, core), space: 32 (over y, z, x_lo).
Axes of the slice: x: 4 (x_hi: 2, x_lo: 2; x = x_hi * 2 + x_lo), y: 4, z: 4, core: 2. Of those that a mesh axis runs over, the one named last changes fastest.
Arguments:
- adjoint: bfloat16 [8, 5, 512, 32, 256], P('inst', None, 'space'), may hold values from -6 to 6
- flux_terms: bfloat16 [8, 5, 3, 512, 32, 256], P('inst', None, None, 'space'), may hold values from -6 to 6
- stiffness: float32 [512, 32, 256], P('space', 'inst'), may hold values from 0.1 to 1
- normals: float32 [3, 512, 32], P(None, 'space', 'inst'), may hold values from -6 to 6
- design_map: int32 [512, 32], P('space', 'inst'), may hold values from 0 to 1023
Outputs:
- mesh_adjoint: float32 [3, 512, 32, 256], P(None, 'space', 'inst')
- design_grad: float32 [1024], P(('inst', 'space'))
All inputs are finite; a program needn't handle non-finite values.
Results may differ from a plain program's by a relative error of at most 0.00075.
Values sent between devices are 32-bit elements; how exact they have to be, the bound alone decides.
A program may use at most 64 MiB of HBM per device.

v0:
```python
import jax
import jax.numpy as jnp
from jax import lax
from jax.sharding import PartitionSpec as P

SWEEPS = 2
DV_DEV = 8


def with_halo(block, sides, width):
    for axis, dim in sides:
        count = lax.axis_size(axis)
        forward = [(i, i + 1) for i in range(count - 1)]
        backward = [(target, source) for source, target in forward]
        low = lax.ppermute(
            lax.slice_in_dim(block, block.shape[dim] - width, None, axis=dim), axis, forward
        )
        high = lax.ppermute(lax.slice_in_dim(block, 0, width, axis=dim), axis, backward)
        block = jnp.concatenate([low, block, high], axis=dim)
    return block


def pad_third(padded):
    return jnp.pad(padded, ((0, 0), (0, 0), (0, 0), (1, 1)))


def inner_metric(grown):
    padded = pad_third(grown)
    first = padded[0, :-2, 1:-1, 1:-1] - padded[0, 2:, 1:-1, 1:-1]
    second = padded[1, 1:-1, :-2, 1:-1] - padded[1, 1:-1, 2:, 1:-1]
    third = padded[2, 1:-1, 1:-1, :-2] - padded[2, 1:-1, 1:-1, 2:]
    return grown[:, 1:-1, 1:-1, :] + 0.5 * jnp.stack([first, second, third])


def inner_neighbours(grown):
    padded = pad_third(grown)
    summed = padded[:, :-2, 1:-1, 1:-1] + padded[:, 2:, 1:-1, 1:-1]
    summed = summed + padded[:, 1:-1, :-2, 1:-1] + padded[:, 1:-1, 2:, 1:-1]
    summed = summed + padded[:, 1:-1, 1:-1, :-2] + padded[:, 1:-1, 1:-1, 2:]
    return summed


def metric_full(weighted):
    return inner_metric(with_halo(weighted, (("inst", 2), ("space", 1)), 1))


def sweep_full(field):
    return inner_neighbours(with_halo(field, (("inst", 2), ("space", 1)), 1))


def per_device(adjoint, flux_terms, stiffness, normals, design_map):
    instance_count = adjoint.shape[0] * lax.axis_size("inst")
    partial_work = (
        jnp.einsum("kvxyz,kvdxyz->dxyz", adjoint, flux_terms, preferred_element_type=jnp.float32)
        / instance_count
    )
    weighted = lax.psum_scatter(partial_work, "inst", scatter_dimension=2, tiled=True)
    diagonal = 6.5 * stiffness
    volume_grad = metric_full(weighted)
    mesh_adjoint = volume_grad / diagonal
    for sweep_index in range(SWEEPS):
        mesh_adjoint = (volume_grad + sweep_full(stiffness * mesh_adjoint)) / diagonal
    surface = jnp.sum(normals * mesh_adjoint[:, :, :, 0], axis=0)
    flat_values = surface.reshape(-1)
    flat_ids = design_map.reshape(-1)
    design_total = DV_DEV * lax.axis_size("inst") * lax.axis_size("space")
    one_hot = (flat_ids[:, None] == jnp.arange(design_total, dtype=jnp.int32)[None, :]).astype(
        jnp.float32
    )
    partial_design = jnp.dot(flat_values, one_hot, precision=lax.Precision.HIGHEST)
    design_grad = lax.psum_scatter(
        partial_design, ("inst", "space"), scatter_dimension=0, tiled=True
    )
    return (mesh_adjoint, design_grad)


def solution(mesh):
    in_specs = (
        P("inst", None, "space", None, None),
        P("inst", None, None, "space", None, None),
        P("space", "inst", None),
        P(None, "space", "inst"),
        P("space", "inst"),
    )
    out_specs = (P(None, "space", "inst", None), P(("inst", "space")))
    return jax.shard_map(
        per_device, mesh=mesh, in_specs=in_specs, out_specs=out_specs, check_vma=False
    )
```

profile of v0, /device:TPU:1, one launch (start us, length us, event | category | flops | bytes accessed | tf_op | source)
XLA Modules:
  0.0 194.2 jit_solution(17043629852306655073)
XLA Ops:
  7.2 0.0 reduce-scatter.2.cloned.1.call-start
  7.2 2.4 %bitcast_convert_fusion = f32[16,32,256,2,5]{2,1,0,4,3:T(8,128)S(1)} fusion(bf16[2,5,16,32,256]{4,3,2,1,0:T(8,128)(2,1)} %param.5), kind=kLoop, calls=%fused_computation.1 | loop fusion | flops 1310720 | bytes 7864320
  9.6 6.9 %multiply_reduce_fusion = f32[16,32,256,3]{2,1,0,3:T(8,128)} fusion(f32[16,32,256,2,5]{2,1,0,4,3:T(8,128)S(1)} %bitcast_convert_fusion, bf16[2,5,3,16,32,256]{5,4,3,2,1,0:T(8,128)(2,1)} %param.6), kind=kLoop, calls=%fused_computation | loop fusion | flops 11403264 | bytes 14680064 | tf_op jit(solution)/shard_map/kvxyz,kvdxyz->dxyz/dot_general | solution.py:54
  16.5 2.8 %multiply_bitcast_fusion = f32[3,16,32,256]{3,2,1,0:T(8,128)} fusion(f32[16,32,256,3]{2,1,0,3:T(8,128)} %multiply_reduce_fusion), kind=kLoop, calls=%fused_computation.6 | loop fusion | flops 393216 | bytes 3145728 | tf_op jit(solution)/shard_map/div | solution.py:54
  19.3 38.1 %reduce-scatter.2.cloned.1.call-done = f32[3,16,8,256]{3,2,1,0:T(8,128)} async-done(((f32[3,16,32,256]{3,2,1,0:T(8,128)}), f32[3,16,8,256]{3,2,1,0:T(8,128)}) %reduce-scatter.2.cloned.1.call-update) | async-done | bytes 393232 | tf_op jit(solution)/shard_map/reduce_scatter | solution.py:57
  57.4 1.2 fusion.22
  58.6 2.7 %collective-permute-start = (f32[3,16,1,256]{3,2,1,0:T(1,128)S(1)}, f32[3,16,1,256]{3,2,1,0:T(1,128)S(1)}, u32[]{:S(2)}, u32[]{:S(2)}) collective-permute-start(f32[3,16,1,256]{3,2,1,0:T(1,128)S(1)} %get-tuple-element.20), channel_id=1, source_target_pairs={{0,32},{32,64},{64,96},{1,33},{33,65},{65,97},{2,34},{34,66},{66,9... | collective-permute-start | bytes 147464 | tf_op jit(solution)/shard_map/ppermute | solution.py:15
  61.3 1.9 collective-permute-start.1
  63.3 1.1 copy.204
  64.4 3.8 %collective-permute-done.1 = f32[3,16,1,256]{3,2,1,0:T(1,128)S(1)} collective-permute-done((f32[3,16,1,256]{3,2,1,0:T(1,128)S(1)}, f32[3,16,1,256]{3,2,1,0:T(1,128)S(1)}, u32[]{:S(2)}, u32[]{:S(2)}) %collective-permute-start.1) | collective-permute-done | bytes 49184 | tf_op jit(solution)/shard_map/ppermute | solution.py:18
  68.2 0.1 pad_maximum_fusion
  68.4 3.3 %collective-permute-start.2 = (f32[3,1,10,256]{3,1,2,0:T(1,128)S(1)}, f32[3,1,10,256]{3,1,2,0:T(1,128)S(1)}, u32[]{:S(2)}, u32[]{:S(2)}) collective-permute-start(f32[3,1,10,256]{3,1,2,0:T(1,128)S(1)} %copy.197), channel_id=1, source_target_pairs={{0,1},{1,2},{2,3},{3,4},{4,5},{5,6},{6,7},{7,8},{8,9},{9,10},{10,1... | collective-permute-start | bytes 92168 | tf_op jit(solution)/shard_map/ppermute | solution.py:15
  71.8 1.3 collective-permute-start.3
  73.1 0.3 copy.199
  73.5 0.3 copy.207
  73.8 0.1 copy.209
  73.9 2.5 %collective-permute-done.3 = f32[3,1,10,256]{3,1,2,0:T(1,128)S(1)} collective-permute-done((f32[3,1,10,256]{3,1,2,0:T(1,128)S(1)}, f32[3,1,10,256]{3,1,2,0:T(1,128)S(1)}, u32[]{:S(2)}, u32[]{:S(2)}) %collective-permute-start.3) | collective-permute-done | bytes 30752 | tf_op jit(solution)/shard_map/ppermute | solution.py:18
  76.4 0.1 fusion.17
  76.6 0.6 select_maximum_fusion.8
  77.2 0.1 slice_subtract_fusion
  77.3 0.1 copy.210
  77.4 0.1 divide_multiply_fusion
  77.5 0.1 fusion.21
  77.5 3.9 %collective-permute-start.4 = (f32[3,16,1,256]{3,2,1,0:T(1,128)S(1)}, f32[3,16,1,256]{3,2,1,0:T(1,128)S(1)}, u32[]{:S(2)}, u32[]{:S(2)}) collective-permute-start(f32[3,16,1,256]{3,2,1,0:T(1,128)S(1)} %get-tuple-element.18), channel_id=1, source_target_pairs={{0,32},{32,64},{64,96},{1,33},{33,65},{65,97},{2,34},{34,66},{66,9... | collective-permute-start | bytes 147464 | tf_op jit(solution)/shard_map/ppermute | solution.py:15
  81.5 1.9 collective-permute-start.5
  83.4 5.0 %collective-permute-done.5 = f32[3,16,1,256]{3,2,1,0:T(1,128)S(1)} collective-permute-done((f32[3,16,1,256]{3,2,1,0:T(1,128)S(1)}, f32[3,16,1,256]{3,2,1,0:T(1,128)S(1)}, u32[]{:S(2)}, u32[]{:S(2)}) %collective-permute-start.5) | collective-permute-done | bytes 49184 | tf_op jit(solution)/shard_map/ppermute | solution.py:18
  88.5 3.0 %collective-permute-start.6 = (f32[3,1,10,256]{3,1,2,0:T(1,128)S(1)}, f32[3,1,10,256]{3,1,2,0:T(1,128)S(1)}, u32[]{:S(2)}, u32[]{:S(2)}) collective-permute-start(f32[3,1,10,256]{3,1,2,0:T(1,128)S(1)} %copy.211), channel_id=1, source_target_pairs={{0,1},{1,2},{2,3},{3,4},{4,5},{5,6},{6,7},{7,8},{8,9},{9,10},{10,1... | collective-permute-start | bytes 92168 | tf_op jit(solution)/shard_map/ppermute | solution.py:15
  91.5 1.3 collective-permute-start.7
  92.9 3.3 %collective-permute-done.7 = f32[3,1,10,256]{3,1,2,0:T(1,128)S(1)} collective-permute-done((f32[3,1,10,256]{3,1,2,0:T(1,128)S(1)}, f32[3,1,10,256]{3,1,2,0:T(1,128)S(1)}, u32[]{:S(2)}, u32[]{:S(2)}) %collective-permute-start.7) | collective-permute-done | bytes 30752 | tf_op jit(solution)/shard_map/ppermute | solution.py:18
  96.2 0.8 select_maximum_fusion.4
  97.0 0.5 fusion.10
  97.4 0.1 fusion.20
  97.5 3.8 %collective-permute-start.8 = (f32[3,16,1,256]{3,2,1,0:T(1,128)S(1)}, f32[3,16,1,256]{3,2,1,0:T(1,128)S(1)}, u32[]{:S(2)}, u32[]{:S(2)}) collective-permute-start(f32[3,16,1,256]{3,2,1,0:T(1,128)S(1)} %get-tuple-element.16), channel_id=1, source_target_pairs={{0,32},{32,64},{64,96},{1,33},{33,65},{65,97},{2,34},{34,66},{66,9... | collective-permute-start | bytes 147464 | tf_op jit(solution)/shard_map/ppermute | solution.py:15
  101.3 1.9 collective-permute-start.9
  103.2 5.0 %collective-permute-done.9 = f32[3,16,1,256]{3,2,1,0:T(1,128)S(1)} collective-permute-done((f32[3,16,1,256]{3,2,1,0:T(1,128)S(1)}, f32[3,16,1,256]{3,2,1,0:T(1,128)S(1)}, u32[]{:S(2)}, u32[]{:S(2)}) %collective-permute-start.9) | collective-permute-done | bytes 49184 | tf_op jit(solution)/shard_map/ppermute | solution.py:18
  108.3 3.4 %collective-permute-start.10 = (f32[3,1,10,256]{3,1,2,0:T(1,128)S(1)}, f32[3,1,10,256]{3,1,2,0:T(1,128)S(1)}, u32[]{:S(2)}, u32[]{:S(2)}) collective-permute-start(f32[3,1,10,256]{3,1,2,0:T(1,128)S(1)} %copy.217), channel_id=1, source_target_pairs={{0,1},{1,2},{2,3},{3,4},{4,5},{5,6},{6,7},{7,8},{8,9},{9,10},{10,1... | collective-permute-start | bytes 92168 | tf_op jit(solution)/shard_map/ppermute | solution.py:15
  111.7 1.3 collective-permute-start.11
  113.0 0.1 copy.225
  113.1 0.1 eq.15
  113.2 3.1 %collective-permute-done.11 = f32[3,1,10,256]{3,1,2,0:T(1,128)S(1)} collective-permute-done((f32[3,1,10,256]{3,1,2,0:T(1,128)S(1)}, f32[3,1,10,256]{3,1,2,0:T(1,128)S(1)}, u32[]{:S(2)}, u32[]{:S(2)}) %collective-permute-start.11) | collective-permute-done | bytes 30752 | tf_op jit(solution)/shard_map/ppermute | solution.py:18
  116.4 0.8 select_maximum_fusion
  117.2 0.4 fusion.4
  117.6 0.2 copy.223
  117.9 0.1 copy.224
  118.0 0.1 reshape.13
  118.1 0.3 fusion.2
  118.4 68.4 %all-reduce.3 = f32[1024]{0:T(1024)S(1)} all-reduce(f32[1024]{0:T(1024)S(1)} %bitcast.12), channel_id=3, replica_groups=mesh['inst'=4,'space'=32] {'inst','space'}, use_global_device_ids=true, to_apply=%region_2.3.clone | all-reduce | flops 1024 | bytes 8192
  186.8 0.6 dynamic-slice
  (39 shorter events, 0.5 us)
Async XLA Ops:
  7.2 50.2 %reduce-scatter.2.cloned.1.call-start = ((), (), s32[]{:S(2)}) async-start(), calls=%async_computation.1 | async-start | bytes 1966080 | tf_op jit(solution)/shard_map/reduce_scatter | solution.py:57
  19.3 44.0 %copy-start.1 = (f32[16,8,256]{2,1,0:T(8,128)S(1)}, f32[16,8,256]{2,1,0:T(8,128)}, u32[]{:S(2)}) copy-start(f32[16,8,256]{2,1,0:T(8,128)} %param.7) | copy-start | bytes 393220
  57.4 10.9 %copy-start = (f32[3,16,8,256]{3,2,1,0:T(8,128)S(1)}, f32[3,16,8,256]{3,2,1,0:T(8,128)}, u32[]{:S(2)}) copy-start(f32[3,16,8,256]{3,2,1,0:T(8,128)} %reduce-scatter.2.cloned.1.call-done) | copy-start | bytes 1179652
  58.6 5.8 %collective-permute-start = (f32[3,16,1,256]{3,2,1,0:T(1,128)S(1)}, f32[3,16,1,256]{3,2,1,0:T(1,128)S(1)}, u32[]{:S(2)}, u32[]{:S(2)}) collective-permute-start(f32[3,16,1,256]{3,2,1,0:T(1,128)S(1)} %get-tuple-element.20), channel_id=1, source_target_pairs={{0,32},{32,64},{64,96},{1,33},{33,65},{65,97},{2,34},{34,66},{66,9... | collective-permute-start | bytes 147464 | tf_op jit(solution)/shard_map/ppermute | solution.py:15
  61.3 6.9 %collective-permute-start.1 = (f32[3,16,1,256]{3,2,1,0:T(1,128)S(1)}, f32[3,16,1,256]{3,2,1,0:T(1,128)S(1)}, u32[]{:S(2)}, u32[]{:S(2)}) collective-permute-start(f32[3,16,1,256]{3,2,1,0:T(1,128)S(1)} %get-tuple-element.21), channel_id=1, source_target_pairs={{32,0},{64,32},{96,64},{33,1},{65,33},{97,65},{34,2},{66,34},{98,6... | collective-permute-start | bytes 147464 | tf_op jit(solution)/shard_map/ppermute | solution.py:18
  68.4 5.4 %collective-permute-start.2 = (f32[3,1,10,256]{3,1,2,0:T(1,128)S(1)}, f32[3,1,10,256]{3,1,2,0:T(1,128)S(1)}, u32[]{:S(2)}, u32[]{:S(2)}) collective-permute-start(f32[3,1,10,256]{3,1,2,0:T(1,128)S(1)} %copy.197), channel_id=1, source_target_pairs={{0,1},{1,2},{2,3},{3,4},{4,5},{5,6},{6,7},{7,8},{8,9},{9,10},{10,1... | collective-permute-start | bytes 92168 | tf_op jit(solution)/shard_map/ppermute | solution.py:15
  71.8 4.6 %collective-permute-start.3 = (f32[3,1,10,256]{3,1,2,0:T(1,128)S(1)}, f32[3,1,10,256]{3,1,2,0:T(1,128)S(1)}, u32[]{:S(2)}, u32[]{:S(2)}) collective-permute-start(f32[3,1,10,256]{3,1,2,0:T(1,128)S(1)} %copy.200), channel_id=1, source_target_pairs={{1,0},{2,1},{3,2},{4,3},{5,4},{6,5},{7,6},{8,7},{9,8},{10,9},{11,1... | collective-permute-start | bytes 92168 | tf_op jit(solution)/shard_map/ppermute | solution.py:18
  77.5 5.9 %collective-permute-start.4 = (f32[3,16,1,256]{3,2,1,0:T(1,128)S(1)}, f32[3,16,1,256]{3,2,1,0:T(1,128)S(1)}, u32[]{:S(2)}, u32[]{:S(2)}) collective-permute-start(f32[3,16,1,256]{3,2,1,0:T(1,128)S(1)} %get-tuple-element.18), channel_id=1, source_target_pairs={{0,32},{32,64},{64,96},{1,33},{33,65},{65,97},{2,34},{34,66},{66,9... | collective-permute-start | bytes 147464 | tf_op jit(solution)/shard_map/ppermute | solution.py:15
  81.5 6.9 %collective-permute-start.5 = (f32[3,16,1,256]{3,2,1,0:T(1,128)S(1)}, f32[3,16,1,256]{3,2,1,0:T(1,128)S(1)}, u32[]{:S(2)}, u32[]{:S(2)}) collective-permute-start(f32[3,16,1,256]{3,2,1,0:T(1,128)S(1)} %get-tuple-element.19), channel_id=1, source_target_pairs={{32,0},{64,32},{96,64},{33,1},{65,33},{97,65},{34,2},{66,34},{98,6... | collective-permute-start | bytes 147464 | tf_op jit(solution)/shard_map/ppermute | solution.py:18
  88.5 4.4 %collective-permute-start.6 = (f32[3,1,10,256]{3,1,2,0:T(1,128)S(1)}, f32[3,1,10,256]{3,1,2,0:T(1,128)S(1)}, u32[]{:S(2)}, u32[]{:S(2)}) collective-permute-start(f32[3,1,10,256]{3,1,2,0:T(1,128)S(1)} %copy.211), channel_id=1, source_target_pairs={{0,1},{1,2},{2,3},{3,4},{4,5},{5,6},{6,7},{7,8},{8,9},{9,10},{10,1... | collective-permute-start | bytes 92168 | tf_op jit(solution)/shard_map/ppermute | solution.py:15
  91.5 4.6 %collective-permute-start.7 = (f32[3,1,10,256]{3,1,2,0:T(1,128)S(1)}, f32[3,1,10,256]{3,1,2,0:T(1,128)S(1)}, u32[]{:S(2)}, u32[]{:S(2)}) collective-permute-start(f32[3,1,10,256]{3,1,2,0:T(1,128)S(1)} %copy.213), channel_id=1, source_target_pairs={{1,0},{2,1},{3,2},{4,3},{5,4},{6,5},{7,6},{8,7},{9,8},{10,9},{11,1... | collective-permute-start | bytes 92168 | tf_op jit(solution)/shard_map/ppermute | solution.py:18
  97.0 16.1 %copy-start.4 = (s32[16,8]{0,1:T(8,128)S(1)}, s32[16,8]{0,1:T(8,128)}, u32[]{:S(2)}) copy-start(s32[16,8]{0,1:T(8,128)} %param.9) | copy-start | bytes 1540
  97.5 5.7 %collective-permute-start.8 = (f32[3,16,1,256]{3,2,1,0:T(1,128)S(1)}, f32[3,16,1,256]{3,2,1,0:T(1,128)S(1)}, u32[]{:S(2)}, u32[]{:S(2)}) collective-permute-start(f32[3,16,1,256]{3,2,1,0:T(1,128)S(1)} %get-tuple-element.16), channel_id=1, source_target_pairs={{0,32},{32,64},{64,96},{1,33},{33,65},{65,97},{2,34},{34,66},{66,9... | collective-permute-start | bytes 147464 | tf_op jit(solution)/shard_map/ppermute | solution.py:15
  101.3 6.9 %collective-permute-start.9 = (f32[3,16,1,256]{3,2,1,0:T(1,128)S(1)}, f32[3,16,1,256]{3,2,1,0:T(1,128)S(1)}, u32[]{:S(2)}, u32[]{:S(2)}) collective-permute-start(f32[3,16,1,256]{3,2,1,0:T(1,128)S(1)} %get-tuple-element.17), channel_id=1, source_target_pairs={{32,0},{64,32},{96,64},{33,1},{65,33},{97,65},{34,2},{66,34},{98,6... | collective-permute-start | bytes 147464 | tf_op jit(solution)/shard_map/ppermute | solution.py:18
  108.3 4.9 %collective-permute-start.10 = (f32[3,1,10,256]{3,1,2,0:T(1,128)S(1)}, f32[3,1,10,256]{3,1,2,0:T(1,128)S(1)}, u32[]{:S(2)}, u32[]{:S(2)}) collective-permute-start(f32[3,1,10,256]{3,1,2,0:T(1,128)S(1)} %copy.217), channel_id=1, source_target_pairs={{0,1},{1,2},{2,3},{3,4},{4,5},{5,6},{6,7},{7,8},{8,9},{9,10},{10,1... | collective-permute-start | bytes 92168 | tf_op jit(solution)/shard_map/ppermute | solution.py:15
  111.7 4.6 %collective-permute-start.11 = (f32[3,1,10,256]{3,1,2,0:T(1,128)S(1)}, f32[3,1,10,256]{3,1,2,0:T(1,128)S(1)}, u32[]{:S(2)}, u32[]{:S(2)}) collective-permute-start(f32[3,1,10,256]{3,1,2,0:T(1,128)S(1)} %copy.219), channel_id=1, source_target_pairs={{1,0},{2,1},{3,2},{4,3},{5,4},{6,5},{7,6},{8,7},{9,8},{10,9},{11,1... | collective-permute-start | bytes 92168 | tf_op jit(solution)/shard_map/ppermute | solution.py:18
  117.2 0.7 copy-start.3
  117.6 69.8 %copy-start.2 = (f32[3,16,8,256]{3,2,1,0:T(8,128)}, f32[3,16,8,256]{3,2,1,0:T(8,128)S(1)}, u32[]{:S(2)}) copy-start(f32[3,16,8,256]{3,2,1,0:T(8,128)S(1)} %fusion.4) | copy-start | bytes 1179652
Sparse Core Ops, SparseCore 0:
  19.4 37.8 reduce-scatter.1
where the time goes:
time: 195 us; the launch traced here: 194 us
  blocking collectives  68.4 us (35%)
  waiting for transfers between devices  60.8 us (31%)
  starting transfers between devices  29.8 us (15%)
  other arithmetic  15.6 us (8%)
  between operations  14.5 us (7%)
  local copies, waits for them, and re-layouts  4.75 us (2%)
    unnamed x1, blocking collectives  68.4 us
    reduce_scatter x1, waiting for transfers between devices, per_device(): lax.psum_scatter(partial_work, 'inst', scatter_dimension=2, tiled=True)  38.1 us
    ppermute x6, waiting for transfers between devices, with_halo(): lax.ppermute(lax.slice_in_dim(block, 0, width, axis=dim), axis, backward)  22.7 us
    ppermute x6, starting transfers between devices, with_halo(): lax.ppermute(lax.slice_in_dim(block, block.shape[dim] - width, None, axis...  20.1 us
    ppermute x6, starting transfers between devices, with_halo(): lax.ppermute(lax.slice_in_dim(block, 0, width, axis=dim), axis, backward)  9.64 us
    dot_general x1, other arithmetic, per_device(): jnp.einsum('kvxyz,kvdxyz->dxyz', adjoint, flux_terms, preferred_element_t...  6.87 us
  transfers between devices with their start and end apart: 13, of which 7 were waited for; matrix products, arithmetic and copies ran while one was open for 1% of the time, Pallas kernels for 0%

commit v1 on v0

v1 whole, which is shorter than its diff:
```python
import functools

import jax
import jax.numpy as jnp
from jax import lax
from jax.experimental import pallas as pl
from jax.experimental.pallas import tpu as pltpu
from jax.sharding import PartitionSpec as P

F32 = jnp.float32
MESH = pl.DeviceIdType.MESH
A = 1.0 / 6.5
ROWS = 4
STARTS = (0, 12, 4, 8)
CHUNKS = tuple((zh, x0) for zh in range(2) for x0 in STARTS)
LAG = 3
YZ = 16


def iota(shape, axis):
    return lax.broadcasted_iota(jnp.int32, shape, axis)


def roll(value, shift, axis):
    return pltpu.roll(value, shift % value.shape[axis], axis)


def kernel(
    adj, flux, stiff, normals, dmap, lam_ref, dg_ref,
    av, fv, kv, nv, dv, q, rc, g, xr, ps, pr, w, vg, m1, dsum, ra, rb,
    load_sem, small_sem, c_send, c_recv, x_send, x_recv, h_send, h_recv,
    p_send, p_recv, n_send, n_recv, a_send, a_recv, b_send, b_recv,
):
    inst = lax.axis_index("inst")
    s = lax.axis_index("space")
    h = inst // 2
    c = lax.rem(inst, 2)
    xlo = lax.rem(s, 2)
    yz = s // 2
    partner = (2 * h + 1 - c, s)
    opposite = (2 * (1 - h) + c, s)
    up_dev = (inst, lax.rem(s + 1, 32))
    down_dev = (inst, lax.rem(s + 31, 32))
    has_up = s < 31
    has_down = s > 0
    sends_halo = c == h
    sub = iota((8, 128), 0)
    lane = iota((8, 128), 1)
    zero = jnp.zeros((8, 128), F32)

    loads = []
    for t, (zh, x0) in enumerate(CHUNKS):
        rows, zs = pl.ds(x0, ROWS), pl.ds(zh * 128, 128)
        pair = [
            pltpu.make_async_copy(
                adj.at[:, :, rows, :, zs], av.at[zh, :, :, rows], load_sem.at[t, 0]
            ),
            pltpu.make_async_copy(
                flux.at[:, :, :, rows, :, zs], fv.at[zh, :, :, :, rows], load_sem.at[t, 1]
            ),
        ]
        for copy in pair:
            copy.start()
        loads.append(pair)
    small = [
        pltpu.make_async_copy(stiff, kv, small_sem.at[0]),
        pltpu.make_async_copy(normals, nv, small_sem.at[1]),
        pltpu.make_async_copy(dmap, dv, small_sem.at[2]),
    ]
    for copy in small:
        copy.start()

    def clear(x, _):
        for zh in range(2):
            xr[zh, x, 3] = zero
        return 0

    lax.fori_loop(0, 16, clear, 0)
    for zh in range(2):
        for row in (0, 1, 2, 19, 20, 21):
            for tile in range(6):
                w[zh, row, tile] = zero

    barrier = pltpu.get_barrier_semaphore()

    def signal_yz(j, _):
        target = (inst, lax.rem(yz + j, YZ) * 2 + xlo)
        pl.semaphore_signal(barrier, inc=1, device_id=target, device_id_type=MESH)
        return 0

    lax.fori_loop(1, YZ, signal_yz, 0)
    mine = inst * 2 + xlo

    def x_peer(j):
        other = lax.rem(mine + j, 8)
        return (other // 2, yz * 2 + lax.rem(other, 2))

    for j in range(1, 8):
        pl.semaphore_signal(barrier, inc=1, device_id=x_peer(j), device_id_type=MESH)

    @pl.when(has_up)
    def _():
        pl.semaphore_signal(barrier, inc=1, device_id=up_dev, device_id_type=MESH)

    @pl.when(has_down)
    def _():
        pl.semaphore_signal(barrier, inc=1, device_id=down_dev, device_id_type=MESH)

    def remote(src, dst, send, recv, device):
        return pltpu.make_async_remote_copy(
            src_ref=src, dst_ref=dst, send_sem=send, recv_sem=recv,
            device_id=device, device_id_type=MESH,
        )

    def pack_up(w0, w1, w2):
        return jnp.where(sub < 2, w0, jnp.where(sub < 4, roll(w2, 2, 0), roll(w1, 4, 0)))

    def pack_low(w0, w1, w2):
        return jnp.where(sub >= 6, w0, jnp.where(sub >= 4, roll(w2, 6, 0), roll(w1, 4, 0)))

    def slot(block, core):
        rb = block + h - 2 * block * h
        rk = core + c - 2 * core * c
        return rk * 3 * rb + (1 - rk) * (11 - 4 * rb)

    def core_copy(t):
        zh, x0 = CHUNKS[t]
        rows = pl.ds(x0, ROWS)
        return remote(
            q.at[zh, rows, pl.ds(0, 7)], rc.at[zh, rows], c_send.at[t], c_recv.at[t], partner
        )

    def cross_copy(t):
        zh, x0 = CHUNKS[t]
        rows = pl.ds(x0, ROWS)
        main = pl.ds(0, 3)
        return remote(
            g.at[zh, rows, main], xr.at[zh, rows, main], x_send.at[t], x_recv.at[t], opposite
        )

    def halo_copy(t):
        zh, x0 = CHUNKS[t]
        rows = pl.ds(x0, ROWS)
        last = pl.ds(3, 1)
        return remote(
            g.at[zh, rows, last], xr.at[zh, rows, last], h_send.at[t], h_recv.at[t], opposite
        )

    def pair_copy(t):
        zh, x0 = CHUNKS[t]
        rows = pl.ds(x0, ROWS)
        return remote(ps.at[zh, rows], pr.at[zh, rows], p_send.at[t], p_recv.at[t], partner)

    def partial(t):
        zh, x0 = CHUNKS[t]
        for copy in loads[t]:
            copy.wait()

        def row(r, _):
            x = x0 + r
            tiles = {}
            for block in range(2):
                ys = pl.ds(16 * block, 16)
                acc = [None] * 3
                for k in range(2):
                    for v in range(5):
                        a = av[zh, k, v, x, ys, :].astype(F32)
                        for d in range(3):
                            term = a * fv[zh, k, v, d, x, ys, :].astype(F32)
                            acc[d] = term if acc[d] is None else acc[d] + term
                for core in range(2):
                    base = slot(block, core)
                    for d in range(3):
                        tile = acc[d][8 * core : 8 * core + 8]
                        tiles[block, core, d] = tile
                        q[zh, x, base + d] = tile
            q[zh, x, 6 + 4 * c] = pack_up(*[tiles[1, 0, d] for d in range(3)])
            q[zh, x, 10 - 4 * c] = pack_low(*[tiles[0, 1, d] for d in range(3)])
            return 0

        lax.fori_loop(0, ROWS, row, 0)
        if t == 0:
            extra = has_up.astype(jnp.int32) + has_down.astype(jnp.int32)
            pl.semaphore_wait(barrier, YZ - 1 + 7 + extra)
        core_copy(t).start()

    def cross(t):
        zh, x0 = CHUNKS[t]
        core_copy(t).wait_recv()

        def row(r, _):
            x = x0 + r
            for d in range(4):
                g[zh, x, d] = q[zh, x, 7 + d] + rc[zh, x, 3 + d]
            return 0

        lax.fori_loop(0, ROWS, row, 0)
        cross_copy(t).start()

        @pl.when(sends_halo)
        def _():
            halo_copy(t).start()

    def finish(t):
        zh, x0 = CHUNKS[t]
        cross_copy(t).wait_recv()

        def row(r, _):
            x = x0 + r
            own = [q[zh, x, 11 + d] + rc[zh, x, d] + xr[zh, x, d] for d in range(3)]
            w[zh, x + 3, 0] = own[0]
            w[zh, x + 3, 2] = own[1]
            w[zh, x + 3, 3] = own[2]
            ps[zh, x] = jnp.where(c == 0, pack_low(*own), pack_up(*own))
            return 0

        lax.fori_loop(0, ROWS, row, 0)
        pair_copy(t).start()

    def halo(t):
        zh, x0 = CHUNKS[t]
        pair_copy(t).wait_recv()

        @pl.when(jnp.logical_not(sends_halo))
        def _():
            halo_copy(t).wait_recv()

        def row(r, _):
            x = x0 + r
            far = jnp.where(sends_halo, zero, g[zh, x, 3] + xr[zh, x, 3])
            near = pr[zh, x]
            top = jnp.where(c == 0, near, far)
            low = jnp.where(c == 0, far, near)
            w[zh, x + 3, 1] = jnp.where(sub < 2, top, jnp.where(sub >= 6, low, 0.0))
            w[zh, x + 3, 4] = jnp.where(
                sub < 3, roll(top, 4, 0), jnp.where(sub >= 5, roll(low, 4, 0), 0.0)
            )
            w[zh, x + 3, 5] = jnp.where(
                sub < 2, roll(top, 6, 0), jnp.where(sub >= 6, roll(low, 2, 0), 0.0)
            )
            return 0

        lax.fori_loop(0, ROWS, row, 0)

    def side_copies(zh, side):
        out = []
        for j, width in enumerate((6, 5, 1)):
            src = 18 - j if side == 0 else 3 + j
            dst = 2 - j if side == 0 else 19 + j
            tiles = pl.ds(0, width)
            out.append(
                remote(
                    w.at[zh, src, tiles], w.at[zh, dst, tiles],
                    n_send.at[zh, side, j], n_recv.at[zh, side, j],
                    up_dev if side == 0 else down_dev,
                )
            )
        return out

    def side_send(zh):
        for side, there in ((0, has_up), (1, has_down)):
            @pl.when(there)
            def _(side=side):
                for copy in side_copies(zh, side):
                    copy.start()

    def side_wait(zh):
        for side, there in ((0, has_down), (1, has_up)):
            @pl.when(there)
            def _(side=side):
                for copy in side_copies(zh, side):
                    copy.wait_recv()

    up_ok = (inst < 3).astype(F32)
    low_ok = (inst > 0).astype(F32)
    ring_mask = jnp.where(sub < 4, up_ok, low_ok)
    x_low_ok = has_down.astype(F32)
    x_up_ok = has_up.astype(F32)

    def x_mask(row):
        return jnp.where(row < 3, x_low_ok, jnp.where(row > 18, x_up_ok, 1.0))

    def y_before(own, ring):
        a, b = roll(own, 1, 0), roll(ring, 1, 0)
        return jnp.where(sub == 0, b, a), jnp.where(sub == 0, a, b)

    def y_after(own, ring):
        a, b = roll(own, 7, 0), roll(ring, 7, 0)
        return jnp.where(sub == 7, b, a), jnp.where(sub == 7, a, b)

    def z_before(parts):
        turned = [roll(p, 1, 1) for p in parts]
        return [
            jnp.where(lane == 0, turned[z - 1] if z else 0.0, turned[z]) for z in range(len(parts))
        ]

    def z_after(parts):
        turned = [roll(p, 127, 1) for p in parts]
        last = len(parts) - 1
        return [
            jnp.where(lane == 127, turned[z + 1] if z < last else 0.0, turned[z])
            for z in range(len(parts))
        ]

    own_at = (0, 2, 3)
    ring_at = (1, 4, 5)

    def gradient(halves):
        zs = range(halves)

        def row(x, _):
            xm = x_mask(x)
            rm = ring_mask * xm
            for tile, at in ((0, own_at), (1, ring_at)):
                m = xm if tile == 0 else rm
                for z in zs:
                    mid = w[z, x, at[0]]
                    diff = w[z, x - 1, at[0]] - w[z, x + 1, at[0]]
                    vg[z, x, 0, tile] = (mid + 0.5 * diff) * m
                parts = [w[z, x, at[2]] for z in zs]
                before, after = z_before(parts), z_after(parts)
                for z in zs:
                    vg[z, x, 2, tile] = (parts[z] + 0.5 * (before[z] - after[z])) * m
            for z in zs:
                own, ring = w[z, x, own_at[1]], w[z, x, ring_at[1]]
                before, after = y_before(own, ring), y_after(own, ring)
                vg[z, x, 1, 0] = (own + 0.5 * (before[0] - after[0])) * xm
                vg[z, x, 1, 1] = (ring + 0.5 * (before[1] - after[1])) * rm
            return 0

        lax.fori_loop(1, 21, row, 0)

    def around(ref, x, d, zs, tiles):
        own = [ref[z, x, d, 0] for z in zs]
        ring = [ref[z, x, d, 1] for z in zs]
        total = {}
        for z in zs:
            before, after = y_before(own[z], ring[z]), y_after(own[z], ring[z])
            for tile in tiles:
                total[z, tile] = (
                    before[tile] + after[tile] + ref[z, x - 1, d, tile] + ref[z, x + 1, d, tile]
                )
        for tile in tiles:
            parts = own if tile == 0 else ring
            before, after = z_before(parts), z_after(parts)
            for z in zs:
                total[z, tile] = total[z, tile] + before[z] + after[z]
        return total

    def sweep(halves):
        zs = range(halves)

        def row(x, _):
            xm = x_mask(x) * A
            rm = ring_mask * xm
            for d in range(3):
                total = around(vg, x, d, zs, (0, 1))
                for z in zs:
                    m1[z, x, d, 0] = (vg[z, x, d, 0] + A * total[z, 0]) * xm
                    m1[z, x, d, 1] = (vg[z, x, d, 1] + A * total[z, 1]) * rm
            return 0

        lax.fori_loop(2, 20, row, 0)

    def last_sweep(x, halves):
        zs = range(halves)
        out = [[None] * 3 for _ in zs]
        for z in zs:
            out[z] = [None] * 3
        scale = [0.125 / (6.5 * kv[x, :, 128 * z : 128 * z + 128]) for z in zs]
        for d in range(3):
            total = around(m1, x + 3, d, zs, (0,))
            for z in zs:
                out[z][d] = (vg[z, x + 3, d, 0] + total[z, 0]) * scale[z]
        return out

    def yz_copy(j):
        target = (inst, lax.rem(yz + j, YZ) * 2 + xlo)
        return remote(dsum.at[0], ra.at[j], a_send.at[j], a_recv.at[j], target)

    def x_copy(j):
        return remote(dsum.at[1], rb.at[j], b_send.at[j], b_recv.at[j], x_peer(j))

    def design_start():
        gradient(1)
        sweep(1)
        small[0].wait()

        def row(x, wall):
            lam = last_sweep(x, 1)[0]
            return tuple(
                jnp.where(lane == x, jnp.broadcast_to(lam[d][:, 0:1], (8, 128)), wall[d])
                for d in range(3)
            )

        wall = lax.fori_loop(0, 16, row, (zero, zero, zero))
        small[1].wait()
        small[2].wait()
        surface = sum(nv[d] * wall[d][:, :16] for d in range(3))
        ids = dv[...]
        values = jnp.concatenate([surface[y : y + 1, :] for y in range(8)], axis=1)
        flat = jnp.concatenate([ids[y : y + 1, :] for y in range(8)], axis=1)
        high, low = flat // 128, lax.rem(flat, 128)
        left = jnp.where(
            jnp.broadcast_to(high, (8, 128)) == sub, jnp.broadcast_to(values, (8, 128)), 0.0
        )
        right = (jnp.broadcast_to(low, (128, 128)) == iota((128, 128), 0)).astype(F32)
        dsum[0] = lax.dot_general(
            left, right, (((1,), (1,)), ((), ())),
            precision=lax.Precision.HIGHEST, preferred_element_type=F32,
        )

        def send(j, _):
            yz_copy(j).start()
            return 0

        lax.fori_loop(1, YZ, send, 0)

    def design_middle():
        def take(j, total):
            yz_copy(j).wait_recv()
            return total + ra[j]

        dsum[1] = lax.fori_loop(1, YZ, take, dsum[0])
        for j in range(1, 8):
            x_copy(j).start()

    def design_end():
        total = dsum[1]
        for j in range(1, 8):
            x_copy(j).wait_recv()
            total = total + rb[j]
        device = inst * 32 + s
        picked = jnp.where(sub == device // 16, total, 0.0)
        line = jnp.broadcast_to(jnp.sum(picked, axis=0, keepdims=True), (8, 128))
        turned = pltpu.roll(line, lax.rem(128 - lax.rem(device, 16) * 8, 128), 1)
        dg_ref[...] = turned[0:1, :8]

    count = len(CHUNKS)
    for t in range(count + LAG + 3):
        if t < count:
            partial(t)
        if 0 <= t - 1 < count:
            cross(t - 1)
        if 0 <= t - 1 - LAG < count:
            finish(t - 1 - LAG)
        done = t - 2 - LAG
        if 0 <= done < count:
            halo(done)
            if done % 4 == 1:
                side_send(done // 4)
            if done == 3:
                side_wait(0)
                design_start()
            if done == 6:
                design_middle()
    side_wait(1)
    gradient(2)
    sweep(2)

    def emit(x, _):
        lam = last_sweep(x, 2)
        for z in range(2):
            for d in range(3):
                lam_ref[d, x, :, 128 * z : 128 * z + 128] = lam[z][d]
        return 0

    lax.fori_loop(0, 16, emit, 0)
    design_end()

    for t in range(count):
        core_copy(t).wait_send()
        cross_copy(t).wait_send()
        pair_copy(t).wait_send()

    @pl.when(sends_halo)
    def _():
        for t in range(count):
            halo_copy(t).wait_send()

    for zh in range(2):
        for side, there in ((0, has_up), (1, has_down)):
            @pl.when(there)
            def _(zh=zh, side=side):
                for copy in side_copies(zh, side):
                    copy.wait_send()

    def drain(j, _):
        yz_copy(j).wait_send()
        return 0

    lax.fori_loop(1, YZ, drain, 0)
    for j in range(1, 8):
        x_copy(j).wait_send()


def per_device(adjoint, flux_terms, stiffness, normals, design_map):
    hbm = pl.BlockSpec(memory_space=pl.ANY)
    dma = pltpu.SemaphoreType.DMA
    count = len(CHUNKS)

    def tiles(*lead):
        return pltpu.VMEM(lead + (8, 128), F32)

    lam, grad = pl.pallas_call(
        kernel,
        out_shape=(
            jax.ShapeDtypeStruct((3, 16, 8, 256), F32),
            jax.ShapeDtypeStruct((1, 8), F32),
        ),
        in_specs=[hbm] * 5,
        out_specs=(
            pl.BlockSpec(memory_space=pltpu.VMEM),
            pl.BlockSpec(memory_space=pltpu.VMEM),
        ),
        scratch_shapes=[
            pltpu.VMEM((2, 2, 5, 16, 32, 128), jnp.bfloat16),
            pltpu.VMEM((2, 2, 5, 3, 16, 32, 128), jnp.bfloat16),
            pltpu.VMEM((16, 8, 256), F32),
            pltpu.VMEM((3, 8, 16), F32),
            pltpu.VMEM((8, 16), jnp.int32),
            tiles(2, 16, 14),
            tiles(2, 16, 7),
            tiles(2, 16, 4),
            tiles(2, 16, 4),
            tiles(2, 16),
            tiles(2, 16),
            tiles(2, 22, 6),
            tiles(2, 22, 3, 2),
            tiles(2, 22, 3, 2),
            tiles(2),
            tiles(YZ),
            tiles(8),
            dma((count, 2)),
            dma((3,)),
            dma((count,)), dma((count,)), dma((count,)), dma((count,)),
            dma((count,)), dma((count,)), dma((count,)), dma((count,)),
            dma((2, 2, 3)), dma((2, 2, 3)),
            dma((YZ,)), dma((YZ,)), dma((8,)), dma((8,)),
        ],
        compiler_params=pltpu.CompilerParams(
            collective_id=0, has_side_effects=True, vmem_limit_bytes=60 * 1024 * 1024
        ),
    )(adjoint, flux_terms, stiffness, normals.transpose(0, 2, 1), design_map.T)
    return lam, grad.reshape(8)


def solution(mesh):
    in_specs = (
        P("inst", None, "space", None, None),
        P("inst", None, None, "space", None, None),
        P("space", "inst", None),
        P(None, "space", "inst"),
        P("space", "inst"),
    )
    out_specs = (P(None, "space", "inst", None), P(("inst", "space")))
    return jax.shard_map(
        per_device, mesh=mesh, in_specs=in_specs, out_specs=out_specs, check_vma=False
    )
```

time: 195 us -> 43.4 us (0.22)
  blocking collectives: 68.4 us -> 0 us
  waiting for transfers between devices: 60.8 us -> 0 us
  Pallas kernels: 0 us -> 39.5 us
  starting transfers between devices: 29.8 us -> 0 us
  other arithmetic: 15.6 us -> 0 us
  between operations: 14.5 us -> 0.64 us
    unnamed x1 -> x0, blocking collectives: 68.4 us -> none
    pallas_call x0 -> x1, Pallas kernels: none -> 39.5 us  [per_device(): pl.pallas_call(kernel, out_shape=(jax.ShapeDtypeStruct((3, 16, 8, 256), F...]
    reduce_scatter x1 -> x0, waiting for transfers between devices: 38.1 us -> none  [per_device(): lax.psum_scatter(partial_work, 'inst', scatter_dimension=2, tiled=True)]
    ppermute x12 -> x0, starting transfers between devices: 29.8 us -> none  [the longest x6 20.1 us: with_halo(): lax.ppermute(lax.slice_in_dim(block, block.shape[dim] - width, None, axis...]
    ppermute x12 -> x0, waiting for transfers between devices: 22.7 us -> none  [the longest x6 22.7 us: with_halo(): lax.ppermute(lax.slice_in_dim(block, 0, width, axis=dim), axis, backward)]
    dot_general x1 -> x0, other arithmetic: 6.87 us -> none  [per_device(): jnp.einsum('kvxyz,kvdxyz->dxyz', adjoint, flux_terms, preferred_element_t...]
    div x2 -> x0, other arithmetic: 3.19 us -> none  [the longest x1 2.78 us: per_device(): jnp.einsum('kvxyz,kvdxyz->dxyz', adjoint, flux_terms, preferred_element_t...]
    unnamed x1 -> x0, other arithmetic: 2.41 us -> none
  transfers between devices with their start and end apart: 13 -> 0, of which waited for: 7 -> 0; matrix products, arithmetic and copies ran while one was open for 1% -> 0% of each run, Pallas kernels for 0% -> 0%
where the time goes in v1:
time: 43.4 us; the launch traced here: 43 us
  Pallas kernels  39.5 us (91%)
  local copies, waits for them, and re-layouts  2.89 us (7%)
  between operations  0.64 us (1%)
    pallas_call x1, Pallas kernels, per_device(): pl.pallas_call(kernel, out_shape=(jax.ShapeDtypeStruct((3, 16, 8, 256), F...  39.5 us
    unnamed x2, local copies, waits for them, and re-layouts  2.89 us

profile of v1, /device:TPU:1, one launch (start us, length us, event | category | flops | bytes accessed | tf_op | source)
XLA Modules:
  0.0 43.0 jit_solution(2380698757494241666)
XLA Ops:
  0.6 39.5 %shard_map.68 = (f32[3,16,8,256]{3,2,1,0:T(8,128)}, f32[1,8]{1,0:T(1,128)}) custom-call(bf16[2,5,16,32,256]{4,3,2,1,0:T(8,128)(2,1)} %adj.1, bf16[2,5,3,16,32,256]{5,4,3,2,1,0:T(8,128)(2,1)} %flux.1, f32[16,8,256]{2,1,0:T(8,128)} %stiff.1, f32[3,8,16]{2,1,0:T(8,128)} %bitcast.3, s32[8,16]{1,0:T(8,128)} %bitcast.4), custom_call_target="tpu_custom_call" | custom-call | tf_op jit(solution)/shard_map/pallas_call | solution.py:505
  40.1 1.8 %copy.9 = f32[3,16,8,256]{3,2,1,0:T(8,128)} copy(f32[3,16,8,256]{3,2,1,0:T(8,128)} %get-tuple-element.8) | data formatting | bytes 786432
  41.9 1.1 %copy.10 = f32[8]{0:T(128)} copy(f32[8]{0:T(128)} %bitcast.5) | data formatting | bytes 64

commit v2 on v1

--- a/solution.py
+++ b/solution.py
@@ -15,6 +15,7 @@
 CHUNKS = tuple((zh, x0) for zh in range(2) for x0 in STARTS)
 LAG = 3
 YZ = 16
+REACH = (1, 2, 4, 8)
 
 
 def iota(shape, axis):
@@ -29,7 +30,7 @@
     adj, flux, stiff, normals, dmap, lam_ref, dg_ref,
     av, fv, kv, nv, dv, q, rc, g, xr, ps, pr, w, vg, m1, dsum, ra, rb,
     load_sem, small_sem, c_send, c_recv, x_send, x_recv, h_send, h_recv,
-    p_send, p_recv, n_send, n_recv, a_send, a_recv, b_send, b_recv,
+    p_send, p_recv, n_send, n_recv, a_send, a_recv, b_send, b_recv, ring_sem,
 ):
     inst = lax.axis_index("inst")
     s = lax.axis_index("space")
@@ -83,28 +84,23 @@
 
     barrier = pltpu.get_barrier_semaphore()
 
-    def signal_yz(j, _):
-        target = (inst, lax.rem(yz + j, YZ) * 2 + xlo)
-        pl.semaphore_signal(barrier, inc=1, device_id=target, device_id_type=MESH)
-        return 0
-
-    lax.fori_loop(1, YZ, signal_yz, 0)
+    for device in (partner, opposite, up_dev, down_dev):
+        pl.semaphore_signal(barrier, inc=1, device_id=device, device_id_type=MESH)
     mine = inst * 2 + xlo
 
     def x_peer(j):
         other = lax.rem(mine + j, 8)
         return (other // 2, yz * 2 + lax.rem(other, 2))
 
-    for j in range(1, 8):
-        pl.semaphore_signal(barrier, inc=1, device_id=x_peer(j), device_id_type=MESH)
-
-    @pl.when(has_up)
-    def _():
-        pl.semaphore_signal(barrier, inc=1, device_id=up_dev, device_id_type=MESH)
-
-    @pl.when(has_down)
-    def _():
-        pl.semaphore_signal(barrier, inc=1, device_id=down_dev, device_id_type=MESH)
+    def ring_signal(r):
+        for step in (REACH[r], 32 - REACH[r]):
+            pl.semaphore_signal(
+                ring_sem.at[r], inc=1, device_id=(inst, lax.rem(s + step, 32)),
+                device_id_type=MESH,
+            )
+
+    def ring_wait(r):
+        pl.semaphore_wait(ring_sem.at[r], 2)
 
     def remote(src, dst, send, recv, device):
         return pltpu.make_async_remote_copy(
@@ -180,8 +176,8 @@
 
         lax.fori_loop(0, ROWS, row, 0)
         if t == 0:
-            extra = has_up.astype(jnp.int32) + has_down.astype(jnp.int32)
-            pl.semaphore_wait(barrier, YZ - 1 + 7 + extra)
+            pl.semaphore_wait(barrier, 4)
+            ring_signal(0)
         core_copy(t).start()
 
     def cross(t):
@@ -447,6 +443,10 @@
         done = t - 2 - LAG
         if 0 <= done < count:
             halo(done)
+            if done < 4:
+                ring_wait(done)
+            if done < 3:
+                ring_signal(done + 1)
             if done % 4 == 1:
                 side_send(done // 4)
             if done == 3:
@@ -537,6 +537,7 @@
             dma((count,)), dma((count,)), dma((count,)), dma((count,)),
             dma((2, 2, 3)), dma((2, 2, 3)),
             dma((YZ,)), dma((YZ,)), dma((8,)), dma((8,)),
+            pltpu.SemaphoreType.REGULAR((4,)),
         ],
         compiler_params=pltpu.CompilerParams(
             collective_id=0, has_side_effects=True, vmem_limit_bytes=60 * 1024 * 1024

time: 43.4 us -> 43.4 us (level)
  no operation moved by 1% of the time
where the time goes in v2:
time: 43.4 us; the launch traced here: 43.2 us
  Pallas kernels  39.7 us (91%)
  local copies, waits for them, and re-layouts  2.89 us (7%)
  between operations  0.64 us (1%)
    pallas_call x1, Pallas kernels, per_device(): pl.pallas_call(kernel, out_shape=(jax.ShapeDtypeStruct((3, 16, 8, 256), F...  39.7 us
    unnamed x2, local copies, waits for them, and re-layouts  2.89 us

profile of v2, /device:TPU:1, one launch (start us, length us, event | category | flops | bytes accessed | tf_op | source)
XLA Modules:
  0.0 43.2 jit_solution(13942152482142610744)
XLA Ops:
  0.6 39.7 %shard_map.68 = (f32[3,16,8,256]{3,2,1,0:T(8,128)}, f32[1,8]{1,0:T(1,128)}) custom-call(bf16[2,5,16,32,256]{4,3,2,1,0:T(8,128)(2,1)} %adj.1, bf16[2,5,3,16,32,256]{5,4,3,2,1,0:T(8,128)(2,1)} %flux.1, f32[16,8,256]{2,1,0:T(8,128)} %stiff.1, f32[3,8,16]{2,1,0:T(8,128)} %bitcast.3, s32[8,16]{1,0:T(8,128)} %bitcast.4), custom_call_target="tpu_custom_call" | custom-call | tf_op jit(solution)/shard_map/pallas_call | solution.py:505
  40.3 1.8 %copy.9 = f32[3,16,8,256]{3,2,1,0:T(8,128)} copy(f32[3,16,8,256]{3,2,1,0:T(8,128)} %get-tuple-element.8) | data formatting | bytes 786432
  42.1 1.1 %copy.10 = f32[8]{0:T(128)} copy(f32[8]{0:T(128)} %bitcast.5) | data formatting | bytes 64

commit v3 on v2

--- a/solution.py
+++ b/solution.py
@@ -303,13 +303,14 @@
 
     def gradient(halves):
         zs = range(halves)
+        fresh = range(halves - 1, halves)
 
         def row(x, _):
             xm = x_mask(x)
             rm = ring_mask * xm
             for tile, at in ((0, own_at), (1, ring_at)):
                 m = xm if tile == 0 else rm
-                for z in zs:
+                for z in fresh:
                     mid = w[z, x, at[0]]
                     diff = w[z, x - 1, at[0]] - w[z, x + 1, at[0]]
                     vg[z, x, 0, tile] = (mid + 0.5 * diff) * m
@@ -317,7 +318,7 @@
                 before, after = z_before(parts), z_after(parts)
                 for z in zs:
                     vg[z, x, 2, tile] = (parts[z] + 0.5 * (before[z] - after[z])) * m
-            for z in zs:
+            for z in fresh:
                 own, ring = w[z, x, own_at[1]], w[z, x, ring_at[1]]
                 before, after = y_before(own, ring), y_after(own, ring)
                 vg[z, x, 1, 0] = (own + 0.5 * (before[0] - after[0])) * xm
@@ -449,13 +450,12 @@
                 ring_signal(done + 1)
             if done % 4 == 1:
                 side_send(done // 4)
-            if done == 3:
+            if done == 5:
                 side_wait(0)
                 design_start()
-            if done == 6:
-                design_middle()
     side_wait(1)
     gradient(2)
+    design_middle()
     sweep(2)
 
     def emit(x, _):

time: 43.4 us -> 44.5 us (1.025)
  Pallas kernels: 39.7 us -> 40.8 us
    pallas_call x1, Pallas kernels: 39.7 us -> 40.8 us  [per_device(): pl.pallas_call(kernel, out_shape=(jax.ShapeDtypeStruct((3, 16, 8, 256), F...]
where the time goes in v3:
time: 44.5 us; the launch traced here: 44.3 us
  Pallas kernels  40.8 us (92%)
  local copies, waits for them, and re-layouts  2.89 us (6%)
  between operations  0.64 us (1%)
    pallas_call x1, Pallas kernels, per_device(): pl.pallas_call(kernel, out_shape=(jax.ShapeDtypeStruct((3, 16, 8, 256), F...  40.8 us
    unnamed x2, local copies, waits for them, and re-layouts  2.89 us

profile of v3, /device:TPU:1, one launch (start us, length us, event | category | flops | bytes accessed | tf_op | source)
XLA Modules:
  0.0 44.3 jit_solution(10116505999446737790)
XLA Ops:
  0.6 40.8 %shard_map.68 = (f32[3,16,8,256]{3,2,1,0:T(8,128)}, f32[1,8]{1,0:T(1,128)}) custom-call(bf16[2,5,16,32,256]{4,3,2,1,0:T(8,128)(2,1)} %adj.1, bf16[2,5,3,16,32,256]{5,4,3,2,1,0:T(8,128)(2,1)} %flux.1, f32[16,8,256]{2,1,0:T(8,128)} %stiff.1, f32[3,8,16]{2,1,0:T(8,128)} %bitcast.3, s32[8,16]{1,0:T(8,128)} %bitcast.4), custom_call_target="tpu_custom_call" | custom-call | tf_op jit(solution)/shard_map/pallas_call | solution.py:505
  41.4 1.8 %copy.9 = f32[3,16,8,256]{3,2,1,0:T(8,128)} copy(f32[3,16,8,256]{3,2,1,0:T(8,128)} %get-tuple-element.8) | data formatting | bytes 786432
  43.2 1.1 %copy.10 = f32[8]{0:T(128)} copy(f32[8]{0:T(128)} %bitcast.5) | data formatting | bytes 64
